TPU v7x, 32 devices: a whole 2x2x4 slice. The times are simulated.
32 devices in a mesh: line: 8 (over z, x), row: 4 (over y, core).
Axes of the slice: x: 2, y: 2, z: 4, core: 2. Of those that a mesh axis runs over, the one named last changes fastest.
Arguments:
- scalar_field: float32 [2048, 64, 512], P('line', None, 'row'), may hold values from -24 to 24
- cross_coef: float32 [2048, 64, 512], P('line', None, 'row'), may hold values from 0.03 to 0.24
- coupling: float32 [2048, 64, 512], P('line', None, 'row'), may hold values from 2000 to 20000
Outputs:
- solution: float32 [2048, 64, 512], P('line', None, 'row')
All inputs are finite; a program needn't handle non-finite values.
Results may differ from a plain program's by a relative error of at most 0.003.
Values sent between devices are 32-bit elements; how exact they have to be, the bound alone decides.
A program may use at most 192 MiB of HBM per device.

v0:
```python
import functools

import jax
import jax.numpy as jnp
from jax import lax
from jax.experimental import pallas as pl
from jax.experimental.pallas import tpu as pltpu
from jax.sharding import PartitionSpec as P

F32 = jnp.float32
ANY = pl.BlockSpec(memory_space=pl.ANY)
VMEM = pl.BlockSpec(memory_space=pltpu.VMEM)


def lane_index(shape):
    return lax.broadcasted_iota(jnp.int32, shape, 1)


def pack_kernel(chunks, field, low, high, held, sems):
    points, depth, rows = held.shape
    step = points // chunks
    group = min(rows, points)
    copies = []
    for n in range(chunks):
        span = pl.ds(n * step, step)
        copy = pltpu.make_async_copy(field.at[span], held.at[span], sems.at[n])
        copy.start()
        copies.append(copy)
    lanes = lane_index((depth, rows))
    for n in range(chunks):
        copies[n].wait()
        base = n * step
        block, offset = base // group, base % group

        def body(k, state):
            first, last = state
            place = offset + k
            turned = pltpu.roll(held[base + k], place, 1)
            before = jnp.where(place == 0, rows - 1, place - 1)
            return jnp.where(lanes == place, turned, first), jnp.where(lanes == before, turned, last)

        if offset == 0:
            state = (jnp.zeros((depth, rows), F32), jnp.zeros((depth, rows), F32))
        state = lax.fori_loop(0, step, body, state, unroll=4)
        if offset + step == group:
            low[block], high[block] = state


def pack_edges(field):
    points, depth, rows = field.shape
    chunks = 8
    blocks = max(1, points // rows)
    shape = jax.ShapeDtypeStruct((blocks, depth, rows), F32)
    return pl.pallas_call(
        functools.partial(pack_kernel, chunks),
        out_shape=(shape, shape),
        in_specs=[ANY],
        out_specs=(VMEM, VMEM),
        scratch_shapes=[pltpu.VMEM(field.shape, F32), pltpu.SemaphoreType.DMA((chunks,))],
        name="pack_edges",
    )(field)


def forward_kernel(chunks, field, cross, coupling, following, left, right, g, h, f, ends, turned_left, sems):
    points, depth, rows = g.shape
    step = points // chunks
    group = min(rows, points)
    copies = []
    for n in range(chunks):
        span = pl.ds(n * step, step)
        for m, (source, target) in enumerate(((coupling, f), (field, g), (cross, h))):
            copy = pltpu.make_async_copy(source.at[span], target.at[span], sems.at[3 * n + m])
            copy.start()
            copies.append(copy)
    f[points] = following[...]
    for block in range(left.shape[0]):
        turned_left[block] = pltpu.roll(left[block], 2, 1)
    lanes = lane_index((depth, rows))
    planes = lax.broadcasted_iota(jnp.int32, (depth, rows), 0)

    def body(i, state):
        d, carried, unit, total, square = state
        x = g[i]
        block, k = i // group, lax.rem(i, group)
        later = jnp.where(k == rows - 1, 0, k + 1)
        edge = jnp.where(lanes == k, right[block], turned_left[block])
        edge = pltpu.roll(edge, rows - 1 - k, 1)
        beside = jnp.where(lanes == 0, edge, pltpu.roll(x, 1, 1))
        beside += jnp.where(lanes == rows - 1, edge, pltpu.roll(x, rows - 1, 1))
        beside += jnp.where(planes == 0, 0.0, pltpu.roll(x, 1, 0))
        beside += jnp.where(planes == depth - 1, 0.0, pltpu.roll(x, depth - 1, 0))
        y = (x + h[i] * (beside - 4.0 * x)) + carried
        above = f[i + 1]
        r = 1.0 / (d + above)
        factor = above * r
        part = y * r
        share = unit * r
        f[i] = factor
        g[i] = part
        h[i] = share
        return (
            1.0 + factor * d,
            factor * y,
            unit * factor,
            total + unit * part,
            square + unit * share,
        )

    zero = jnp.zeros((depth, rows), F32)
    state = None
    copies[0].wait()
    first = f[0]
    ends[0] = first
    state = (1.0 + first, zero, first, zero, zero)
    for n in range(chunks):
        if n > 0:
            copies[3 * n].wait()
        copies[3 * n + 1].wait()
        copies[3 * n + 2].wait()
        stop = (n + 1) * step if n + 1 == chunks else (n + 1) * step - 1
        start = max(n * step - 1, 0)
        state = lax.fori_loop(start, stop, body, state)
    d, carried, unit, total, square = state
    scale = 1.0 / ends[0]
    ends[0] = total * scale
    ends[1] = square * scale
    ends[2] = unit * scale
    ends[3] = g[points - 1]
    ends[4] = h[points - 1]
    ends[5] = f[points - 1]


def forward(field, cross, coupling, following, left, right):
    points, depth, rows = field.shape
    chunks = 16
    big = pltpu.VMEM((points, depth, rows), F32)
    return pl.pallas_call(
        functools.partial(forward_kernel, chunks),
        out_shape=(
            big,
            big,
            pltpu.VMEM((points + 1, depth, rows), F32),
            jax.ShapeDtypeStruct((6, depth, rows), F32),
        ),
        in_specs=[ANY, ANY, ANY, VMEM, VMEM, VMEM],
        out_specs=(VMEM, VMEM, VMEM, VMEM),
        scratch_shapes=[pltpu.VMEM(left.shape, F32), pltpu.SemaphoreType.DMA((3 * chunks,))],
        compiler_params=pltpu.CompilerParams(vmem_limit_bytes=8 << 20),
        name="forward",
    )(field, cross, coupling, following, left, right)


def backward_kernel(chunks, g, h, f, beside, out, held, sems):
    points = g.shape[0]
    step = points // chunks
    before = beside[0]

    def body(k, value, top):
        i = top - 1 - k
        value = f[i] * value + (g[i] + h[i] * before)
        held[i] = value
        return value

    value = beside[1]
    copies = []
    for n in reversed(range(chunks)):
        value = lax.fori_loop(0, step, functools.partial(body, top=(n + 1) * step), value, unroll=4)
        span = pl.ds(n * step, step)
        copy = pltpu.make_async_copy(held.at[span], out.at[span], sems.at[n])
        copy.start()
        copies.append(copy)
    for copy in copies:
        copy.wait()


def backward(g, h, f, beside):
    chunks = 16
    return pl.pallas_call(
        functools.partial(backward_kernel, chunks),
        out_shape=jax.ShapeDtypeStruct(g.shape, F32),
        in_specs=[VMEM, VMEM, VMEM, VMEM],
        out_specs=ANY,
        scratch_shapes=[pltpu.VMEM(g.shape, F32), pltpu.SemaphoreType.DMA((chunks,))],
        compiler_params=pltpu.CompilerParams(vmem_limit_bytes=12 << 20),
        name="backward",
    )(g, h, f, beside)


def join(a, b, e, q, p, t):
    count = a.shape[0]
    last, slope = q[0], t[0]
    heads, steep = [a[0]], [e[0]]
    lasts, slopes = [q[0]], [t[0]]
    for j in range(1, count):
        scale = 1.0 / (1.0 - b[j] * slope)
        head = (a[j] + b[j] * last) * scale
        climb = e[j] * scale
        reach = p[j] * slope
        last, slope = q[j] + p[j] * last + reach * head, t[j] + reach * climb
        heads.append(head)
        steep.append(climb)
        lasts.append(last)
        slopes.append(slope)
    following = jnp.zeros_like(a[0])
    before, after = [], []
    for j in reversed(range(count)):
        after.append(following)
        head = heads[j] + steep[j] * following
        before.append(lasts[j - 1] + slopes[j - 1] * head if j else jnp.zeros_like(head))
        following = head
    return jnp.stack([jnp.stack(before[::-1]), jnp.stack(after[::-1])])


def shards(field, cross, coupling):
    points, depth, rows = field.shape
    groups, sides = lax.axis_size("line"), lax.axis_size("row")
    low, high = pack_edges(field)
    left = lax.ppermute(high, "row", [(i, i + 1) for i in range(sides - 1)])
    right = lax.ppermute(low, "row", [(i + 1, i) for i in range(sides - 1)])
    following = lax.ppermute(coupling[0], "line", [((i + 1) % groups, i) for i in range(groups)])
    g, h, f, ends = forward(field, cross, coupling, following, left, right)
    packed = ends.reshape(6, groups, depth // groups, rows)
    gathered = lax.all_to_all(packed, "line", split_axis=1, concat_axis=1, tiled=True)
    pairs = join(*gathered)
    beside = lax.all_to_all(pairs, "line", split_axis=1, concat_axis=1, tiled=True)
    return backward(g, h, f, beside.reshape(2, depth, rows))


def solution(mesh):
    spec = P("line", None, "row")
    return jax.shard_map(
        shards, mesh=mesh, in_specs=(spec, spec, spec), out_specs=spec, check_vma=False
    )
```

profile of v0, /device:TPU:0, one launch (start us, length us, event | category | flops | bytes accessed | tf_op | source)
XLA Modules:
  0.0 107.2 jit_solution(17705954784933863810)
XLA Ops:
  0.0 8.5 %pack_edges.1 = (f32[2,64,128]{2,1,0:T(8,128)}, f32[2,64,128]{2,1,0:T(8,128)}) custom-call(f32[256,64,128]{2,1,0:T(8,128)} %field.3), custom_call_target="tpu_custom_call" | custom-call | tf_op jit(solution)/shard_map/pack_edges/pallas_call | solution.py:54
  8.5 2.4 %collective-permute-start.1 = (f32[2,64,128]{2,1,0:T(8,128)}, f32[2,64,128]{2,1,0:T(8,128)S(1)}, u32[]{:S(2)}, u32[]{:S(2)}) collective-permute-start(f32[2,64,128]{2,1,0:T(8,128)} %get-tuple-element.11), channel_id=1, source_target_pairs={{0,1},{1,2},{2,3},{4,5},{5,6},{6,7},{8,9},{9,10},{10,11},{12,13},{... | collective-permute-start | bytes 196616 | tf_op jit(solution)/shard_map/ppermute | solution.py:218
  10.9 1.3 %collective-permute-start.2 = (f32[2,64,128]{2,1,0:T(8,128)}, f32[2,64,128]{2,1,0:T(8,128)S(1)}, u32[]{:S(2)}, u32[]{:S(2)}) collective-permute-start(f32[2,64,128]{2,1,0:T(8,128)} %get-tuple-element.12), channel_id=1, source_target_pairs={{1,0},{2,1},{3,2},{5,4},{6,5},{7,6},{9,8},{10,9},{11,10},{13,12},{... | collective-permute-start | bytes 196616 | tf_op jit(solution)/shard_map/ppermute | solution.py:219
  12.2 0.8 slice_bitcast_fusion
  12.9 5.3 %collective-permute-start = (f32[64,128]{1,0:T(8,128)S(1)}, f32[64,128]{1,0:T(8,128)S(1)}, u32[]{:S(2)}, u32[]{:S(2)}) collective-permute-start(f32[64,128]{1,0:T(8,128)S(1)} %slice_bitcast_fusion), channel_id=1, source_target_pairs={{4,0},{8,4},{12,8},{16,12},{20,16},{24,20},{28,24},{0,28},{5,1},{9... | collective-permute-start | bytes 98312 | tf_op jit(solution)/shard_map/ppermute | solution.py:220
  18.3 1.6 %collective-permute-done.following = f32[64,128]{1,0:T(8,128)S(1)} collective-permute-done((f32[64,128]{1,0:T(8,128)S(1)}, f32[64,128]{1,0:T(8,128)S(1)}, u32[]{:S(2)}, u32[]{:S(2)}) %collective-permute-start) | collective-permute-done | bytes 32800 | tf_op jit(solution)/shard_map/ppermute | solution.py:220
  19.9 0.0 collective-permute-done.1.left
  19.9 0.0 collective-permute-done.2.right
  19.9 0.0 copy-start
  19.9 3.4 %copy-done = f32[256,64,128]{2,1,0:T(8,128)S(1)} copy-done((f32[256,64,128]{2,1,0:T(8,128)S(1)}, f32[256,64,128]{2,1,0:T(8,128)}, u32[]{:S(2)}) %copy-start) | copy-done | bytes 8388632
  23.3 0.0 copy-start.7
  23.3 3.4 %copy-done.7 = f32[256,64,128]{2,1,0:T(8,128)S(1)} copy-done((f32[256,64,128]{2,1,0:T(8,128)S(1)}, f32[256,64,128]{2,1,0:T(8,128)}, u32[]{:S(2)}) %copy-start.7) | copy-done | bytes 8388632
  26.7 30.6 %forward.1 = (f32[256,64,128]{2,1,0:T(8,128)S(1)}, f32[256,64,128]{2,1,0:T(8,128)S(1)}, f32[257,64,128]{2,1,0:T(8,128)S(1)}, f32[6,64,128]{2,1,0:T(8,128)S(1)}) custom-call(f32[256,64,128]{2,1,0:T(8,128)S(1)} %copy-done, f32[256,64,128]{2,1,0:T(8,128)S(1)} %copy-done.7, f32[256,64,128]{2,1,0:T(8,128)} %coupling.1, ...), custom_call_target="tpu_custom_call" | custom-call | tf_op jit(solution)/shard_map/forward/pallas_call | solution.py:137
  57.2 0.0 copy-start.1
  57.2 3.3 %copy-done.1 = f32[257,64,128]{2,1,0:T(8,128)} copy-done((f32[257,64,128]{2,1,0:T(8,128)}, f32[257,64,128]{2,1,0:T(8,128)S(1)}, u32[]{:S(2)}) %copy-start.1) | copy-done | bytes 8421400
  60.5 0.0 copy-start.3
  60.5 3.4 %copy-done.3 = f32[256,64,128]{2,1,0:T(8,128)} copy-done((f32[256,64,128]{2,1,0:T(8,128)}, f32[256,64,128]{2,1,0:T(8,128)S(1)}, u32[]{:S(2)}) %copy-start.3) | copy-done | bytes 8388632
  63.9 0.0 copy-start.5
  63.9 3.2 %copy-done.5 = f32[256,64,128]{2,1,0:T(8,128)} copy-done((f32[256,64,128]{2,1,0:T(8,128)}, f32[256,64,128]{2,1,0:T(8,128)S(1)}, u32[]{:S(2)}) %copy-start.5) | copy-done | bytes 8388632
  67.1 0.7 copy.4
  67.8 6.3 %all-to-all-start = ((f32[6,8,8,128]{3,2,0,1:T(8,128)}), f32[6,8,8,128]{3,2,0,1:T(8,128)S(1)}, u32[]{:S(2)}, u32[]{:S(2)}) async-start(f32[6,8,8,128]{3,2,0,1:T(8,128)} %copy.4), calls=%async_computation | async-start | bytes 393216 | tf_op jit(solution)/shard_map/all_to_all | solution.py:223
  74.1 9.2 %all-to-all-done = f32[6,8,8,128]{3,2,0,1:T(8,128)S(1)} async-done(((f32[6,8,8,128]{3,2,0,1:T(8,128)}), f32[6,8,8,128]{3,2,0,1:T(8,128)S(1)}, u32[]{:S(2)}, u32[]{:S(2)}) %all-to-all-start) | async-done | bytes 196640 | tf_op jit(solution)/shard_map/all_to_all | solution.py:223
  83.2 0.1 constant_dynamic-update-slice_fusion.6
  83.5 10.1 %all_to_all.10 = f32[2,8,8,128]{3,2,0,1:T(8,128)S(1)} all-to-all(f32[2,8,8,128]{3,2,0,1:T(8,128)S(1)} %copy.45), channel_id=1, replica_groups=mesh['line'=8,'row'=4] {'line'}, dimensions={1} | all-to-all | bytes 131072 | tf_op jit(solution)/shard_map/all_to_all | solution.py:225
  93.5 0.0 copy-start.2
  93.5 3.4 %copy-done.2 = f32[257,64,128]{2,1,0:T(8,128)S(1)} copy-done((f32[257,64,128]{2,1,0:T(8,128)S(1)}, f32[257,64,128]{2,1,0:T(8,128)}, u32[]{:S(2)}) %copy-start.2) | copy-done | bytes 8421400
  96.9 0.0 copy-start.4
  96.9 3.4 %copy-done.4 = f32[256,64,128]{2,1,0:T(8,128)S(1)} copy-done((f32[256,64,128]{2,1,0:T(8,128)S(1)}, f32[256,64,128]{2,1,0:T(8,128)}, u32[]{:S(2)}) %copy-start.4) | copy-done | bytes 8388632
  100.3 0.0 copy-start.6
  100.3 3.4 %copy-done.6 = f32[256,64,128]{2,1,0:T(8,128)S(1)} copy-done((f32[256,64,128]{2,1,0:T(8,128)S(1)}, f32[256,64,128]{2,1,0:T(8,128)}, u32[]{:S(2)}) %copy-start.6) | copy-done | bytes 8388632
  103.7 3.5 %backward.1 = f32[256,64,128]{2,1,0:T(8,128)} custom-call(f32[256,64,128]{2,1,0:T(8,128)S(1)} %copy-done.4, f32[256,64,128]{2,1,0:T(8,128)S(1)} %copy-done.6, f32[257,64,128]{2,1,0:T(8,128)S(1)} %copy-done.2, f32[2,64,128]{2,1,0:T(8,128)S(1)} %bitcast.520), custom_call_target="tpu_custom_call" | custom-call | tf_op jit(solution)/shard_map/backward/pallas_call | solution.py:178
  (12 shorter events, 0.1 us)
Async XLA Ops:
  8.5 11.4 %collective-permute-start.1 = (f32[2,64,128]{2,1,0:T(8,128)}, f32[2,64,128]{2,1,0:T(8,128)S(1)}, u32[]{:S(2)}, u32[]{:S(2)}) collective-permute-start(f32[2,64,128]{2,1,0:T(8,128)} %get-tuple-element.11), channel_id=1, source_target_pairs={{0,1},{1,2},{2,3},{4,5},{5,6},{6,7},{8,9},{9,10},{10,11},{12,13},{... | collective-permute-start | bytes 196616 | tf_op jit(solution)/shard_map/ppermute | solution.py:218
  10.9 9.0 %collective-permute-start.2 = (f32[2,64,128]{2,1,0:T(8,128)}, f32[2,64,128]{2,1,0:T(8,128)S(1)}, u32[]{:S(2)}, u32[]{:S(2)}) collective-permute-start(f32[2,64,128]{2,1,0:T(8,128)} %get-tuple-element.12), channel_id=1, source_target_pairs={{1,0},{2,1},{3,2},{5,4},{6,5},{7,6},{9,8},{10,9},{11,10},{13,12},{... | collective-permute-start | bytes 196616 | tf_op jit(solution)/shard_map/ppermute | solution.py:219
  12.9 6.9 %collective-permute-start = (f32[64,128]{1,0:T(8,128)S(1)}, f32[64,128]{1,0:T(8,128)S(1)}, u32[]{:S(2)}, u32[]{:S(2)}) collective-permute-start(f32[64,128]{1,0:T(8,128)S(1)} %slice_bitcast_fusion), channel_id=1, source_target_pairs={{4,0},{8,4},{12,8},{16,12},{20,16},{24,20},{28,24},{0,28},{5,1},{9... | collective-permute-start | bytes 98312 | tf_op jit(solution)/shard_map/ppermute | solution.py:220
  19.9 3.4 %copy-start = (f32[256,64,128]{2,1,0:T(8,128)S(1)}, f32[256,64,128]{2,1,0:T(8,128)}, u32[]{:S(2)}) copy-start(f32[256,64,128]{2,1,0:T(8,128)} %field.3) | copy-start | bytes 25165828
  23.3 3.4 %copy-start.7 = (f32[256,64,128]{2,1,0:T(8,128)S(1)}, f32[256,64,128]{2,1,0:T(8,128)}, u32[]{:S(2)}) copy-start(f32[256,64,128]{2,1,0:T(8,128)} %cross.1) | copy-start | bytes 25165828
  57.2 3.3 %copy-start.1 = (f32[257,64,128]{2,1,0:T(8,128)}, f32[257,64,128]{2,1,0:T(8,128)S(1)}, u32[]{:S(2)}) copy-start(f32[257,64,128]{2,1,0:T(8,128)S(1)} %get-tuple-element.15.f) | copy-start | bytes 25264132
  60.5 3.4 %copy-start.3 = (f32[256,64,128]{2,1,0:T(8,128)}, f32[256,64,128]{2,1,0:T(8,128)S(1)}, u32[]{:S(2)}) copy-start(f32[256,64,128]{2,1,0:T(8,128)S(1)} %get-tuple-element.13.g) | copy-start | bytes 25165828
  63.9 3.2 %copy-start.5 = (f32[256,64,128]{2,1,0:T(8,128)}, f32[256,64,128]{2,1,0:T(8,128)S(1)}, u32[]{:S(2)}) copy-start(f32[256,64,128]{2,1,0:T(8,128)S(1)} %get-tuple-element.14.h) | copy-start | bytes 25165828
  67.8 15.5 %all-to-all-start = ((f32[6,8,8,128]{3,2,0,1:T(8,128)}), f32[6,8,8,128]{3,2,0,1:T(8,128)S(1)}, u32[]{:S(2)}, u32[]{:S(2)}) async-start(f32[6,8,8,128]{3,2,0,1:T(8,128)} %copy.4), calls=%async_computation | async-start | bytes 393216 | tf_op jit(solution)/shard_map/all_to_all | solution.py:223
  93.5 3.4 %copy-start.2 = (f32[257,64,128]{2,1,0:T(8,128)S(1)}, f32[257,64,128]{2,1,0:T(8,128)}, u32[]{:S(2)}) copy-start(f32[257,64,128]{2,1,0:T(8,128)} %copy-done.1) | copy-start | bytes 25264132
  96.9 3.4 %copy-start.4 = (f32[256,64,128]{2,1,0:T(8,128)S(1)}, f32[256,64,128]{2,1,0:T(8,128)}, u32[]{:S(2)}) copy-start(f32[256,64,128]{2,1,0:T(8,128)} %copy-done.3) | copy-start | bytes 25165828
  100.3 3.4 %copy-start.6 = (f32[256,64,128]{2,1,0:T(8,128)S(1)}, f32[256,64,128]{2,1,0:T(8,128)}, u32[]{:S(2)}) copy-start(f32[256,64,128]{2,1,0:T(8,128)} %copy-done.5) | copy-start | bytes 25165828
where the time goes:
time: 108 us; the launch traced here: 107 us
  Pallas kernels  42.5 us (39%)
  local copies, waits for them, and re-layouts  28.2 us (26%)
  starting transfers between devices  15.3 us (14%)
  waiting for transfers between devices  10.8 us (10%)
  blocking collectives  10.1 us (9%)
    pallas_call x1, Pallas kernels, forward(): pl.pallas_call(functools.partial(forward_kernel, chunks), out_shape=(big,...  30.6 us
    unnamed x18, local copies, waits for them, and re-layouts  26.8 us
    all_to_all x1, blocking collectives, shards(): lax.all_to_all(pairs, 'line', split_axis=1, concat_axis=1, tiled=True)  10.1 us
    all_to_all x1, waiting for transfers between devices, shards(): lax.all_to_all(packed, 'line', split_axis=1, concat_axis=1, tiled=True)  9.17 us
    pallas_call x1, Pallas kernels, pack_edges(): pl.pallas_call(functools.partial(pack_kernel, chunks), out_shape=(shape,...  8.46 us
    all_to_all x1, starting transfers between devices, shards(): lax.all_to_all(packed, 'line', split_axis=1, concat_axis=1, tiled=True)  6.29 us
    ppermute x1, starting transfers between devices, shards(): lax.ppermute(coupling[0], 'line', [((i + 1) % groups, i) for i in range(g...  5.35 us
    pallas_call x1, Pallas kernels, backward(): pl.pallas_call(functools.partial(backward_kernel, chunks), out_shape=jax....  3.51 us
  transfers between devices with their start and end apart: 4, of which 2 were waited for; matrix products, arithmetic and copies ran while one was open for 1% of the time, Pallas kernels for 0%

commit v1 on v0

v1 whole, which is shorter than its diff:
```python
import functools

import jax
import jax.numpy as jnp
from jax import lax
from jax.experimental import pallas as pl
from jax.experimental.pallas import tpu as pltpu
from jax.sharding import PartitionSpec as P

F32 = jnp.float32
ANY = pl.BlockSpec(memory_space=pl.ANY)
VMEM = pl.BlockSpec(memory_space=pltpu.VMEM)


def lane_index(shape):
    return lax.broadcasted_iota(jnp.int32, shape, 1)


def join(a, b, e, q, p, t):
    count = len(a)
    last, slope = q[0], t[0]
    heads, steep = [a[0]], [e[0]]
    lasts, slopes = [q[0]], [t[0]]
    for j in range(1, count):
        scale = 1.0 / (1.0 - b[j] * slope)
        head = (a[j] + b[j] * last) * scale
        climb = e[j] * scale
        reach = p[j] * slope
        last, slope = q[j] + p[j] * last + reach * head, t[j] + reach * climb
        heads.append(head)
        steep.append(climb)
        lasts.append(last)
        slopes.append(slope)
    following = jnp.zeros_like(a[0])
    before, after = [], []
    for j in reversed(range(count)):
        after.append(following)
        head = heads[j] + steep[j] * following
        before.append(lasts[j - 1] + slopes[j - 1] * head if j else jnp.zeros_like(head))
        following = head
    return before[::-1], after[::-1]


def remote(source, target, send, recv, device):
    return pltpu.make_async_remote_copy(
        src_ref=source,
        dst_ref=target,
        send_sem=send,
        recv_sem=recv,
        device_id=device,
        device_id_type=pl.DeviceIdType.MESH,
    )


def fetch(source, target, sems, chunks):
    step = target.shape[0] // chunks
    copies = []
    for n in range(chunks):
        span = pl.ds(n * step, step)
        copies.append(pltpu.make_async_copy(source.at[span], target.at[span], sems.at[n]))
    return copies


def pack(held, low, high, copies):
    points, depth, rows = held.shape
    chunks = len(copies)
    step = points // chunks
    group = min(rows, points)
    lanes = lane_index((depth, rows))
    for n in range(chunks):
        copies[n].wait()
        base = n * step
        block, offset = base // group, base % group

        def body(k, state):
            first, last = state
            place = offset + k
            turned = pltpu.roll(held[base + k], place, 1)
            before = jnp.where(place == 0, rows - 1, place - 1)
            return jnp.where(lanes == place, turned, first), jnp.where(lanes == before, turned, last)

        if offset == 0:
            state = (jnp.zeros((depth, rows), F32), jnp.zeros((depth, rows), F32))
        state = lax.fori_loop(0, step, body, state, unroll=4)
        if offset + step == group:
            low[block], high[block] = state


def forward_kernel(
    chunks, groups, sides, field, cross, coupling, g, h, f, beside, held, inverse, low, high,
    left, right, following, ends, got, answer, land, field_sems, cross_sems, coupling_sems,
    edge_sems, out_send, out_recv, back_send, back_recv,
):
    points, depth, rows = g.shape
    step = points // chunks
    group = min(rows, points)
    part_depth = depth // groups
    me, side = lax.axis_index("line"), lax.axis_index("row")
    field_copies = fetch(field, g, field_sems, chunks)
    cross_copies = fetch(cross, held, cross_sems, chunks)
    coupling_copies = []
    for n in range(chunks):
        span = pl.ds(n * step, step)
        coupling_copies.append(
            pltpu.make_async_copy(coupling.at[span], f.at[span], coupling_sems.at[n])
        )
    for copy in field_copies + coupling_copies + cross_copies:
        copy.start()

    above_side = {"row": lax.rem(side + 1, sides)}
    below_side = {"row": lax.rem(side + sides - 1, sides)}
    peers = [lax.rem(me + o, groups) for o in range(1, groups)]
    barrier = pltpu.get_barrier_semaphore()
    for device in [{"line": peer} for peer in peers] + [above_side, below_side]:
        pl.semaphore_signal(barrier, inc=1, device_id=device, device_id_type=pl.DeviceIdType.MESH)
    pl.semaphore_wait(barrier, groups + 1)

    face = remote(coupling.at[0], following, edge_sems.at[0], edge_sems.at[1], {"line": peers[-1]})
    face.start()
    pack(g, low, high, field_copies)
    up = remote(high, left, edge_sems.at[2], edge_sems.at[3], above_side)
    down = remote(low, right, edge_sems.at[4], edge_sems.at[5], below_side)
    up.start()
    down.start()

    def factors(i, state):
        d, unit, square = state
        above = f[i + 1]
        r = 1.0 / (d + above)
        factor = above * r
        share = unit * r
        f[i] = factor
        inverse[i] = r
        h[i] = share
        return 1.0 + factor * d, unit * factor, square + unit * share

    zero = jnp.zeros((depth, rows), F32)
    coupling_copies[0].wait()
    first = f[0]
    beside[0] = first
    state = (1.0 + first, first, zero)
    for n in range(chunks):
        if n > 0:
            coupling_copies[n].wait()
        start = max(n * step - 1, 0)
        state = lax.fori_loop(start, (n + 1) * step - 1, factors, state)
    face.wait()
    f[points] = following[...]
    d, unit, square = factors(points - 1, state)
    scale = 1.0 / beside[0]

    def put(v, value):
        for j in range(groups):
            ends[j, v] = value[j * part_depth : (j + 1) * part_depth]

    put(1, square * scale)
    put(2, unit * scale)
    put(4, h[points - 1])
    put(5, f[points - 1])

    up.wait()
    down.wait()
    for block in range(left.shape[0]):
        left[block] = jnp.where(side == 0, 0.0, pltpu.roll(left[block], 2, 1))
        right[block] = jnp.where(side == sides - 1, 0.0, right[block])
    lanes = lane_index((depth, rows))
    planes = lax.broadcasted_iota(jnp.int32, (depth, rows), 0)

    def sources(i, state):
        carried, total = state
        x = g[i]
        block, k = i // group, lax.rem(i, group)
        edge = jnp.where(lanes == k, right[block], left[block])
        edge = pltpu.roll(edge, rows - 1 - k, 1)
        around = jnp.where(lanes == 0, edge, pltpu.roll(x, 1, 1))
        around += jnp.where(lanes == rows - 1, edge, pltpu.roll(x, rows - 1, 1))
        around += jnp.where(planes == 0, 0.0, pltpu.roll(x, 1, 0))
        around += jnp.where(planes == depth - 1, 0.0, pltpu.roll(x, depth - 1, 0))
        y = (x + held[i] * (around - 4.0 * x)) + carried
        g[i] = y * inverse[i]
        return f[i] * y, total + h[i] * y

    state = (zero, zero)
    for n in range(chunks):
        cross_copies[n].wait()
        state = lax.fori_loop(n * step, (n + 1) * step, sources, state)
    put(0, state[1] * (1.0 / beside[0]))
    put(3, g[points - 1])

    sent = []
    for o, peer in enumerate(peers):
        copy = remote(ends.at[peer], got.at[me], out_send.at[o], out_recv.at[o], {"line": peer})
        copy.start()
        sent.append(copy)
    got[me] = ends[me]
    for copy in sent:
        copy.wait()
    pairs = join(*[[got[j, v] for j in range(groups)] for v in range(6)])
    for j in range(groups):
        answer[j, 0] = pairs[0][j]
        answer[j, 1] = pairs[1][j]
    sent = []
    for o, peer in enumerate(peers):
        copy = remote(answer.at[peer], land.at[me], back_send.at[o], back_recv.at[o], {"line": peer})
        copy.start()
        sent.append(copy)
    land[me] = answer[me]
    for copy in sent:
        copy.wait()
    for j in range(groups):
        for v in range(2):
            beside[v, j * part_depth : (j + 1) * part_depth] = land[j, v]


def forward(field, cross, coupling):
    points, depth, rows = field.shape
    groups, sides = lax.axis_size("line"), lax.axis_size("row")
    chunks = 8
    big = pltpu.VMEM((points, depth, rows), F32)
    edge = pltpu.VMEM((max(1, points // rows), depth, rows), F32)
    part = depth // groups
    dma = pltpu.SemaphoreType.DMA
    return pl.pallas_call(
        functools.partial(forward_kernel, chunks, groups, sides),
        out_shape=(
            big,
            big,
            pltpu.VMEM((points + 1, depth, rows), F32),
            pltpu.VMEM((2, depth, rows), F32),
        ),
        in_specs=[ANY, ANY, ANY],
        out_specs=(VMEM, VMEM, VMEM, VMEM),
        scratch_shapes=[
            big,
            big,
            edge,
            edge,
            edge,
            edge,
            pltpu.VMEM((depth, rows), F32),
            pltpu.VMEM((groups, 6, part, rows), F32),
            pltpu.VMEM((groups, 6, part, rows), F32),
            pltpu.VMEM((groups, 2, part, rows), F32),
            pltpu.VMEM((groups, 2, part, rows), F32),
            dma((chunks,)),
            dma((chunks,)),
            dma((chunks,)),
            dma((6,)),
            dma((groups - 1,)),
            dma((groups - 1,)),
            dma((groups - 1,)),
            dma((groups - 1,)),
        ],
        compiler_params=pltpu.CompilerParams(
            vmem_limit_bytes=28 << 20, collective_id=0, has_side_effects=True
        ),
        name="forward",
    )(field, cross, coupling)


def backward_kernel(chunks, g, h, f, beside, out, held, sems):
    points = g.shape[0]
    step = points // chunks
    before = beside[0]

    def body(k, value, top):
        i = top - 1 - k
        value = f[i] * value + (g[i] + h[i] * before)
        held[i] = value
        return value

    value = beside[1]
    copies = []
    for n in reversed(range(chunks)):
        value = lax.fori_loop(0, step, functools.partial(body, top=(n + 1) * step), value, unroll=4)
        span = pl.ds(n * step, step)
        copy = pltpu.make_async_copy(held.at[span], out.at[span], sems.at[n])
        copy.start()
        copies.append(copy)
    for copy in copies:
        copy.wait()


def backward(g, h, f, beside):
    chunks = 16
    return pl.pallas_call(
        functools.partial(backward_kernel, chunks),
        out_shape=jax.ShapeDtypeStruct(g.shape, F32),
        in_specs=[VMEM, VMEM, VMEM, VMEM],
        out_specs=ANY,
        scratch_shapes=[pltpu.VMEM(g.shape, F32), pltpu.SemaphoreType.DMA((chunks,))],
        compiler_params=pltpu.CompilerParams(vmem_limit_bytes=12 << 20),
        name="backward",
    )(g, h, f, beside)


def shards(field, cross, coupling):
    return backward(*forward(field, cross, coupling))


def solution(mesh):
    spec = P("line", None, "row")
    return jax.shard_map(
        shards, mesh=mesh, in_specs=(spec, spec, spec), out_specs=spec, check_vma=False
    )
```

time: 108 us -> 61.3 us (0.57)
  local copies, waits for them, and re-layouts: 28.2 us -> 0 us
  Pallas kernels: 42.5 us -> 61.1 us
  starting transfers between devices: 15.3 us -> 0 us
  waiting for transfers between devices: 10.8 us -> 0 us
  blocking collectives: 10.1 us -> 0 us
    unnamed x18 -> x0, local copies, waits for them, and re-layouts: 26.8 us -> none
    pallas_call x2 -> x1, Pallas kernels: 39 us -> 57.6 us  [forward(): pl.pallas_call(functools.partial(forward_kernel, chunks, groups, sides),...]
    all_to_all x1 -> x0, blocking collectives: 10.1 us -> none  [shards(): lax.all_to_all(pairs, 'line', split_axis=1, concat_axis=1, tiled=True)]
    all_to_all x1 -> x0, waiting for transfers between devices: 9.17 us -> none  [shards(): lax.all_to_all(packed, 'line', split_axis=1, concat_axis=1, tiled=True)]
    ppermute x3 -> x0, starting transfers between devices: 9.04 us -> none  [the longest x1 5.35 us: shards(): lax.ppermute(coupling[0], 'line', [((i + 1) % groups, i) for i in range(g...]
    all_to_all x1 -> x0, starting transfers between devices: 6.29 us -> none  [shards(): lax.all_to_all(packed, 'line', split_axis=1, concat_axis=1, tiled=True)]
    ppermute x3 -> x0, waiting for transfers between devices: 1.6 us -> none  [the longest x1 1.6 us: shards(): lax.ppermute(coupling[0], 'line', [((i + 1) % groups, i) for i in range(g...]
  transfers between devices with their start and end apart: 4 -> 0, of which waited for: 2 -> 0; matrix products, arithmetic and copies ran while one was open for 1% -> 0% of each run, Pallas kernels for 0% -> 0%
where the time goes in v1:
time: 61.3 us; the launch traced here: 61.1 us
  Pallas kernels  61.1 us (100%)
    pallas_call x1, Pallas kernels, forward(): pl.pallas_call(functools.partial(forward_kernel, chunks, groups, sides),...  57.6 us
    pallas_call x1, Pallas kernels, backward(): pl.pallas_call(functools.partial(backward_kernel, chunks), out_shape=jax....  3.52 us

profile of v1, /device:TPU:0, one launch (start us, length us, event | category | flops | bytes accessed | tf_op | source)
XLA Modules:
  0.0 61.1 jit_solution(17947775381224099228)
XLA Ops:
  0.0 57.6 %forward.1 = (f32[256,64,128]{2,1,0:T(8,128)S(1)}, f32[256,64,128]{2,1,0:T(8,128)S(1)}, f32[257,64,128]{2,1,0:T(8,128)S(1)}, f32[2,64,128]{2,1,0:T(8,128)S(1)}) custom-call(f32[256,64,128]{2,1,0:T(8,128)} %field.1, f32[256,64,128]{2,1,0:T(8,128)} %cross.1, f32[256,64,128]{2,1,0:T(8,128)} %coupling.1), custom_call_target="tpu_custom_call" | custom-call | tf_op jit(solution)/shard_map/forward/pallas_call | solution.py:223
  57.6 3.5 %backward.1 = f32[256,64,128]{2,1,0:T(8,128)} custom-call(f32[256,64,128]{2,1,0:T(8,128)S(1)} %get-tuple-element.9.g, f32[256,64,128]{2,1,0:T(8,128)S(1)} %get-tuple-element.10.h, f32[257,64,128]{2,1,0:T(8,128)S(1)} %get-tuple-element.11.f, f32[2,64,128]{2,1,0:T(8,128)S(1)} %get-tuple-element.12.beside), custom_call_target="tpu_custom_call" | custom-call | tf_op jit(solution)/shard_map/backward/pallas_call | solution.py:286
